TPU v7x, 256 devices: a whole 4x4x8 slice. The times are simulated.
256 devices in a mesh: wide: 64 (over z, y, core), narrow: 4 (over x).
Axes of the slice: x: 4, y: 4, z: 8, core: 2. Of those that a mesh axis runs over, the one named last changes fastest.
Arguments:
- stored_amps: float32 [1024, 16384], P('wide', 'narrow'), may hold values from -6 to 6
- integrals: float32 [16384, 16384], P('narrow', 'wide'), may hold values from -0.046875 to 0.046875
- pair_counts: int32 [4], replicated, may hold values from 2048 to 4096, as said below
- block_map: int32 [64], replicated, may hold values from 0 to 63, each once
Outputs:
- cycle_out: float32 [1024, 16384], P('wide', 'narrow')
Inputs may be any that keep to these rules, and one draw needn't show every extreme that they name: `pair_counts`: each count lies between half of 4096 and 4096; one count equals 4096. `block_map`: a permutation of the indices of wide.
All inputs are finite; a program needn't handle non-finite values.
Results may differ from a plain program's by a relative error of at most 0.000086.
Values sent between devices are 32-bit elements; how exact they have to be, the bound alone decides.
No kernel may reach another device: no remote copies, remote signals or barrier semaphores. Data moves between devices by JAX's collectives and lax.ppermute only.
A program may use at most 64 MiB of HBM per device.

v0:
```python
import jax
import jax.numpy as jnp
from jax import lax
from jax.sharding import PartitionSpec as P

PB = 4096
BR = 8


def true_order(rows_block, block_map, count_wide):
    total = rows_block.shape[0]
    width = rows_block.shape[1]
    slots = total // (count_wide * BR)
    shaped = rows_block.reshape(count_wide, slots, BR, width)
    shaped = jnp.take(shaped, block_map, axis=0)
    return jnp.transpose(shaped, (1, 0, 2, 3)).reshape(total, width)


def on_device(stored_amps, integrals, pair_counts, block_map):
    count_wide = lax.axis_size("wide")
    count_narrow = lax.axis_size("narrow")
    layer = lax.axis_index("narrow")
    width = stored_amps.shape[1]
    columns = layer * width + jnp.arange(width, dtype=jnp.int32)
    owner = columns // PB
    limit = jnp.sum(
        jnp.where(
            owner[:, None] == jnp.arange(4, dtype=jnp.int32)[None, :], pair_counts[None, :], 0
        ),
        axis=1,
    )
    masked = jnp.where((columns % PB < limit)[None, :], stored_amps, jnp.float32(0.0))
    local_cols = integrals.shape[1]
    cycle = jnp.dot(
        lax.all_gather(masked, "wide", axis=0, tiled=True),
        integrals,
        precision=lax.Precision.HIGHEST,
        preferred_element_type=jnp.float32,
    )
    ordered = true_order(cycle, block_map, count_wide)
    moved = lax.all_to_all(ordered, "wide", split_axis=0, concat_axis=1, tiled=True)
    height = moved.shape[0]
    group = local_cols // count_narrow
    moved = moved.reshape(height, count_wide, count_narrow, group)
    moved = jnp.transpose(moved, (0, 2, 1, 3)).reshape(height, count_wide * local_cols)
    cycle_out = lax.psum_scatter(moved, "narrow", scatter_dimension=1, tiled=True)
    return cycle_out


def solution(mesh):
    placed = (P("wide", "narrow"), P("narrow", "wide"), P(), P())
    return jax.shard_map(
        on_device, mesh=mesh, in_specs=placed, out_specs=P("wide", "narrow"), check_vma=False
    )
```

profile of v0, /device:TPU:8, one launch (start us, length us, event | category | flops | bytes accessed | tf_op | source)
XLA Modules:
  0.0 200.3 jit_solution(17723670310562345288)
XLA Ops:
  6.5 0.0 all-gather.2.cloned.1.call-start
  6.6 0.8 select_reduce_fusion
  7.4 1.7 broadcast_select_fusion
  9.0 0.0 all-gather.2.cloned.1.call-update
  9.1 0.0 reduce-scatter.2.cloned.1.call-start
  9.1 0.7 compare_select_fusion
  9.8 0.7 compare_and_fusion
  10.4 100.6 %all-gather.2.cloned.1.call-done = f32[1024,4096]{1,0:T(8,128)} async-done(((f32[16,4096]{1,0:T(8,128)}), f32[1024,4096]{1,0:T(8,128)}) %all-gather.2.cloned.1.call-update) | async-done | bytes 16777232 | tf_op jit(solution)/shard_map/all_gather | solution.py:35
  111.0 16.2 %fusion.6 = f32[1024,256]{1,0:T(8,128)S(1)} fusion(f32[1024,4096]{1,0:T(8,128)} %all-gather.2.cloned.1.call-done, f32[4096,256]{1,0:T(8,128)} %param.5), kind=kOutput, calls=%fused_computation.21 | convolution fusion | flops 12884901888 | bytes 22020096 | tf_op jit(solution)/shard_map/dot_general | solution.py:34
  127.2 0.6 gather_fusion
  127.9 0.1 select_bitcast_fusion
  128.0 0.1 copy.9
  128.1 36.1 %all_to_all.16 = f32[64,16,256]{2,1,0:T(8,128)S(1)} all-to-all(f32[64,16,256]{2,1,0:T(8,128)S(1)} %bitcast.11), channel_id=1, replica_groups=mesh['wide'=64,'narrow'=4] {'wide'}, dimensions={0} | all-to-all | bytes 2097152 | tf_op jit(solution)/shard_map/all_to_all | solution.py:41
  164.2 0.6 copy.10
  164.8 0.9 reshape.59
  165.7 1.7 copy.11
  167.4 3.2 %reshape.60 = f32[16,16384]{1,0:T(8,128)} reshape(f32[16,4,64,64]{3,2,1,0:T(8,128)} %copy.11) | data formatting | bytes 2097152 | tf_op jit(solution)/shard_map/reshape | solution.py:45
  170.6 0.0 reduce-scatter.2.cloned.1.call-update
  170.6 22.9 %reduce-scatter.2.cloned.1.call-done = f32[16,4096]{1,0:T(8,128)} async-done(((f32[16,16384]{1,0:T(8,128)}), f32[16,4096]{1,0:T(8,128)}) %reduce-scatter.2.cloned.1.call-update) | async-done | bytes 262160 | tf_op jit(solution)/shard_map/reduce_scatter | solution.py:46
  (3 shorter events, 0.0 us)
Async XLA Ops:
  6.5 104.5 %all-gather.2.cloned.1.call-start = ((), (), s32[]{:S(2)}) async-start(), calls=%async_computation.2 | async-start | bytes 17039360 | tf_op jit(solution)/shard_map/all_gather | solution.py:35
  9.1 184.4 %reduce-scatter.2.cloned.1.call-start = ((), (), s32[]{:S(2)}) async-start(), calls=%async_computation.3 | async-start | bytes 1310720 | tf_op jit(solution)/shard_map/reduce_scatter | solution.py:46
Sparse Core Ops, SparseCore 0:
  10.1 100.8 all-gather.1
  170.7 22.6 reduce-scatter.1
where the time goes:
time: 201 us; the launch traced here: 200 us
  waiting for transfers between devices  123 us (61%)
  blocking collectives  36.1 us (18%)
  matrix products  16.2 us (8%)
  between operations  13.5 us (7%)
  local copies, waits for them, and re-layouts  7.09 us (4%)
  other arithmetic  3.96 us (2%)
    all_gather x1, waiting for transfers between devices, on_device(): lax.all_gather(masked, 'wide', axis=0, tiled=True)  101 us
    all_to_all x1, blocking collectives, on_device(): lax.all_to_all(ordered, 'wide', split_axis=0, concat_axis=1, tiled=True)  36.1 us
    reduce_scatter x1, waiting for transfers between devices, on_device(): lax.psum_scatter(moved, 'narrow', scatter_dimension=1, tiled=True)  22.9 us
    dot_general x1, matrix products, on_device(): jnp.dot(lax.all_gather(masked, 'wide', axis=0, tiled=True), integrals, pr...  16.2 us
  transfers between devices with their start and end apart: 2, of which 2 were waited for; matrix products, arithmetic and copies ran while one was open for 1% of the time, Pallas kernels for 0%

commit v1 on v0

--- a/solution.py
+++ b/solution.py
@@ -32,7 +32,9 @@
     masked = jnp.where((columns % PB < limit)[None, :], stored_amps, jnp.float32(0.0))
     local_cols = integrals.shape[1]
     cycle = jnp.dot(
-        lax.all_gather(masked, "wide", axis=0, tiled=True),
+        jnp.concatenate(
+            lax.all_to_all(jnp.stack([masked] * lax.axis_size("wide")), "wide", 0, 0), axis=0
+        ),
         integrals,
         precision=lax.Precision.HIGHEST,
         preferred_element_type=jnp.float32,

time: 201 us -> 491 us (2.44)
  waiting for transfers between devices: 123 us -> 392 us
  starting transfers between devices: 0.04 us -> 12.5 us
  local copies, waits for them, and re-layouts: 7.09 us -> 14.9 us
    all_to_all x0 -> x1, waiting for transfers between devices: none -> 369 us  [on_device(): lax.all_to_all(jnp.stack([masked] * lax.axis_size('wide')), 'wide', 0, 0)]
    all_gather x1 -> x0, waiting for transfers between devices: 101 us -> none  [on_device(): lax.all_gather(masked, 'wide', axis=0, tiled=True)]
    all_to_all x0 -> x1, starting transfers between devices: none -> 12.4 us  [on_device(): lax.all_to_all(jnp.stack([masked] * lax.axis_size('wide')), 'wide', 0, 0)]
    another operation x0 -> x1, local copies, waits for them, and re-layouts: none -> 7.8 us  [on_device(): jnp.stack([masked] * lax.axis_size('wide'))]
  transfers between devices with their start and end apart: 2 -> 2, of which waited for: 2 -> 2; matrix products, arithmetic and copies ran while one was open for 1% -> 0% of each run, Pallas kernels for 0% -> 0%
where the time goes in v1:
time: 491 us
  waiting for transfers between devices  392 us (80%)
  blocking collectives  40.1 us (8%)
  matrix products  16.2 us (3%)
  local copies, waits for them, and re-layouts  14.9 us (3%)
  between operations  13.5 us (3%)
  starting transfers between devices  12.5 us (3%)
    all_to_all x1, waiting for transfers between devices, on_device(): lax.all_to_all(jnp.stack([masked] * lax.axis_size('wide')), 'wide', 0, 0)  369 us
    all_to_all x1, blocking collectives, on_device(): lax.all_to_all(ordered, 'wide', split_axis=0, concat_axis=1, tiled=True)  40.1 us
    reduce_scatter x1, waiting for transfers between devices, on_device(): lax.psum_scatter(moved, 'narrow', scatter_dimension=1, tiled=True)  22.8 us
    dot_general x1, matrix products, on_device(): jnp.dot(jnp.concatenate(lax.all_to_all(jnp.stack([masked] * lax.axis_size...  16.2 us
    all_to_all x1, starting transfers between devices, on_device(): lax.all_to_all(jnp.stack([masked] * lax.axis_size('wide')), 'wide', 0, 0)  12.4 us
  transfers between devices with their start and end apart: 2, of which 2 were waited for; matrix products, arithmetic and copies ran while one was open for 0% of the time, Pallas kernels for 0%

profile of v1, /device:TPU:8, one launch (start us, length us, event | category | flops | bytes accessed | tf_op | source)
XLA Modules:
  0.0 490.6 jit_solution(4500557127652575807)
XLA Ops:
  6.6 0.8 select_reduce_fusion
  7.3 1.0 broadcast_select_fusion
  8.3 7.8 %stack.2 = f32[64,16,4096]{2,1,0:T(8,128)} broadcast(f32[16,4096]{1,0:T(8,128)S(1)} %broadcast_select_fusion), dimensions={1,2} | broadcast | bytes 17039360 | tf_op jit(solution)/shard_map/stack | solution.py:36
  16.1 0.0 copy-start
  16.1 12.4 %all-to-all-start = ((f32[64,16,4096]{2,1,0:T(8,128)}), f32[64,16,4096]{2,1,0:T(8,128)}, u32[]{:S(2)}, u32[]{:S(2)}) async-start(f32[64,16,4096]{2,1,0:T(8,128)} %stack.2), calls=%async_computation | async-start | bytes 33554432 | tf_op jit(solution)/shard_map/all_to_all | solution.py:36
  28.6 0.0 reduce-scatter.2.cloned.1.call-start
  28.6 0.0 copy-done
  28.7 368.7 %all-to-all-done = f32[64,16,4096]{2,1,0:T(8,128)} async-done(((f32[64,16,4096]{2,1,0:T(8,128)}), f32[64,16,4096]{2,1,0:T(8,128)}, u32[]{:S(2)}, u32[]{:S(2)}) %all-to-all-start) | async-done | bytes 16777248 | tf_op jit(solution)/shard_map/all_to_all | solution.py:36
  397.4 16.2 %fusion = f32[64,2,8,256]{3,2,1,0:T(8,128)S(1)} fusion(f32[64,16,4096]{2,1,0:T(8,128)} %all-to-all-done, f32[4096,256]{1,0:T(8,128)} %param.5), kind=kOutput, calls=%fused_computation.1 | convolution fusion | flops 12884901888 | bytes 22020096 | tf_op jit(solution)/shard_map/dot_general | solution.py:34
  413.6 0.6 gather_fusion
  414.2 0.1 select_bitcast_fusion
  414.4 0.1 copy.10
  414.5 40.1 %all_to_all.21 = f32[64,16,256]{2,1,0:T(8,128)S(1)} all-to-all(f32[64,16,256]{2,1,0:T(8,128)S(1)} %bitcast.16), channel_id=1, replica_groups=mesh['wide'=64,'narrow'=4] {'wide'}, dimensions={0} | all-to-all | bytes 2097152 | tf_op jit(solution)/shard_map/all_to_all | solution.py:43
  454.5 0.6 copy.11
  455.1 0.9 reshape.61
  456.0 1.7 copy.12
  457.7 3.2 reshape.62
  460.9 0.0 reduce-scatter.2.cloned.1.call-update
  460.9 22.8 %reduce-scatter.2.cloned.1.call-done = f32[16,4096]{1,0:T(8,128)} async-done(((f32[16,16384]{1,0:T(8,128)}), f32[16,4096]{1,0:T(8,128)}) %reduce-scatter.2.cloned.1.call-update) | async-done | bytes 262160 | tf_op jit(solution)/shard_map/reduce_scatter | solution.py:48
  (5 shorter events, 0.1 us)
Async XLA Ops:
  16.1 12.5 %copy-start = (s32[64]{0:T(128)S(1)}, s32[64]{0:T(128)}, u32[]{:S(2)}) copy-start(s32[64]{0:T(128)} %param.7) | copy-start | bytes 772
  16.1 381.2 %all-to-all-start = ((f32[64,16,4096]{2,1,0:T(8,128)}), f32[64,16,4096]{2,1,0:T(8,128)}, u32[]{:S(2)}, u32[]{:S(2)}) async-start(f32[64,16,4096]{2,1,0:T(8,128)} %stack.2), calls=%async_computation | async-start | bytes 33554432 | tf_op jit(solution)/shard_map/all_to_all | solution.py:36
  28.6 455.2 %reduce-scatter.2.cloned.1.call-start = ((), (), s32[]{:S(2)}) async-start(), calls=%async_computation.3 | async-start | bytes 1310720 | tf_op jit(solution)/shard_map/reduce_scatter | solution.py:48
Sparse Core Ops, SparseCore 0:
  461.1 22.6 reduce-scatter.1
